TPU v7x, 256 devices: a whole 4x4x8 slice. The times are simulated.
256 devices in a mesh: expert: 64 (over y, z, core), hidden: 4 (over x).
Axes of the slice: x: 4, y: 4, z: 8, core: 2. Of those that a mesh axis runs over, the one named last changes fastest.
Arguments:
- tokens: bfloat16 [8192, 4096], P('expert', 'hidden'), may hold values from -6 to 6
- routes: int32 [8192, 8], P('expert'), may hold values from 0 to 63, all different within a row; in each aligned block of 128 rows (0 to 127, 128 to 255, ...) at most 24 rows name the same one
- route_gates: float32 [8192, 8], P('expert'), may hold values from 0.03 to 0.3
- loss_weights: float32 [8192], P('expert'), may hold values from 0.25 to 4
- damping: float32 [1], replicated, may hold values from 1 to 16
- w_gate: bfloat16 [64, 4096, 768], P('expert', None, 'hidden'), may hold values from -0.09375 to 0.09375
- w_up: bfloat16 [64, 4096, 768], P('expert', None, 'hidden'), may hold values from -0.09375 to 0.09375
- direction: bfloat16 [64, 768, 4096], P('expert', 'hidden'), may hold values from -6 to 6
- residual: bfloat16 [64, 768, 4096], P('expert', 'hidden'), may hold values from -6 to 6
Outputs:
- solution_step: bfloat16 [64, 768, 4096], P('expert', 'hidden')
- new_residual: bfloat16 [64, 768, 4096], P('expert', 'hidden')
- new_direction: bfloat16 [64, 768, 4096], P('expert', 'hidden')
Inputs may be any that keep to these rules, and one draw needn't show every extreme that they name: `routes`: each token names 8 different experts. Among the tokens of one index of expert (aligned blocks of 128 rows) no expert is named more than 24 times, and in every draw some block names some expert exactly 24 times.
All inputs are finite; a program needn't handle non-finite values.
Results may differ from a plain program's by a relative error of at most 0.011.
Values may be sent and summed in bfloat16 or wider, within the bound.
A program may use at most 128 MiB of HBM per device.

v0:
```python
import jax
import jax.numpy as jnp
from jax import lax
from jax.sharding import PartitionSpec as P


def per_device(
    tokens, routes, route_gates, loss_weights, damping, w_gate, w_up, direction, residual
):
    experts = lax.axis_size("expert")
    tok_rows, top_routes = routes.shape
    capacity = min(tok_rows, 3 * tok_rows * top_routes // (2 * experts))
    route_count = tok_rows * top_routes
    slot_count = experts * capacity
    flat_routes = routes.reshape(-1)
    one_hot = (flat_routes[:, None] == jnp.arange(experts, dtype=jnp.int32)[None, :]).astype(
        jnp.int32
    )
    earlier = jnp.cumsum(one_hot, axis=0) - one_hot
    position = jnp.sum(earlier * one_hot, axis=1)
    slot_of_route = flat_routes * capacity + position
    route_of_slot = (
        jnp.full((slot_count,), route_count, jnp.int32)
        .at[slot_of_route]
        .set(jnp.arange(route_count, dtype=jnp.int32))
    )
    filled = route_of_slot < route_count
    safe_route = jnp.minimum(route_of_slot, route_count - 1)
    token_of_slot = safe_route // top_routes

    def pack_rows(source_rows, index):
        picked = source_rows[index]
        return jnp.where(filled[:, None], picked, jnp.zeros((), picked.dtype)).reshape(
            experts, capacity, -1
        )

    gate_local = w_gate[0]
    up_local = w_up[0]
    whole_tokens = lax.all_gather(tokens, "hidden", axis=1, tiled=True)
    send_rows = pack_rows(whole_tokens, token_of_slot)
    arrived = lax.all_to_all(send_rows, "expert", split_axis=0, concat_axis=0, tiled=True).reshape(
        slot_count, -1
    )
    pre_gate = jnp.dot(arrived, gate_local, preferred_element_type=jnp.float32)
    pre_up = jnp.dot(arrived, up_local, preferred_element_type=jnp.float32)
    hidden = (jax.nn.silu(pre_gate) * pre_up).astype(jnp.bfloat16)
    hidden_full = lax.all_gather(hidden, "hidden", axis=1, tiled=True)
    search_cols = lax.all_to_all(direction[0], "hidden", split_axis=1, concat_axis=0, tiled=True)
    tangent = jnp.dot(hidden_full, search_cols, preferred_element_type=jnp.float32).astype(
        jnp.bfloat16
    )
    returned = lax.all_to_all(
        tangent.reshape(experts, capacity, -1), "expert", split_axis=0, concat_axis=0, tiled=True
    ).reshape(slot_count, -1)
    per_route = returned[slot_of_route].reshape(tok_rows, top_routes, -1)
    combined = jnp.einsum("tjd,tj->td", per_route.astype(jnp.float32), route_gates)
    scaled = combined * loss_weights[:, None]
    cotangent = (
        (route_gates[:, :, None] * scaled[:, None, :]).astype(jnp.bfloat16).reshape(route_count, -1)
    )
    send_back = pack_rows(cotangent, safe_route)
    back_rows = lax.all_to_all(
        send_back, "expert", split_axis=0, concat_axis=0, tiled=True
    ).reshape(slot_count, -1)
    curvature_cols = lax.dot_general(
        hidden_full, back_rows, (((0,), (0,)), ((), ())), preferred_element_type=jnp.float32
    )
    curvature = lax.all_to_all(curvature_cols, "hidden", split_axis=0, concat_axis=1, tiled=True)
    search = direction[0].astype(jnp.float32)
    resid = residual[0].astype(jnp.float32)
    image = search + curvature / damping[0]
    pq_total, rr_total = lax.psum(
        (jnp.sum(search * image), jnp.sum(resid * resid)), ("expert", "hidden")
    )
    alpha_step = rr_total / pq_total
    updated = resid - alpha_step * image
    rr_new = lax.psum(jnp.sum(updated * updated), ("expert", "hidden"))
    beta_ratio = rr_new / rr_total
    solution_step = (alpha_step * search).astype(jnp.bfloat16)[None]
    new_residual = updated.astype(jnp.bfloat16)[None]
    new_direction = (updated + beta_ratio * search).astype(jnp.bfloat16)[None]
    return (solution_step, new_residual, new_direction)


def solution(mesh):
    return jax.shard_map(
        per_device,
        mesh=mesh,
        in_specs=(
            P("expert", "hidden"),
            P("expert", None),
            P("expert", None),
            P("expert"),
            P(),
            P("expert", None, "hidden"),
            P("expert", None, "hidden"),
            P("expert", "hidden", None),
            P("expert", "hidden", None),
        ),
        out_specs=(
            P("expert", "hidden", None),
            P("expert", "hidden", None),
            P("expert", "hidden", None),
        ),
        check_vma=False,
    )
```

profile of v0, /device:TPU:1, one launch (start us, length us, event | category | flops | bytes accessed | tf_op | source)
XLA Modules:
  0.0 834.8 jit_solution(10602769745563700831)
XLA Ops:
  9.0 18.0 %reduce-window.6 = s32[64,8,128]{2,1,0:T(8,128)S(1)} reduce-window(s32[64,8,128]{2,1,0:T(8,128)S(1)} %fusion.25, s32[]{:T(128)} %constant.30.clone.1), window={size=1x1x128 pad=0_0x0_0x127_0}, to_apply=%region_2.3 | reduce-window | flops 8323072 | bytes 524292 | tf_op jit(solution)/shard_map/reduce-window
  28.5 4.3 scatter_custom_fusion
  33.0 5.2 all-gather.3.cloned.1.call-done
  38.2 23.4 %gather_fusion = bf16[1536,4096]{1,0:T(8,128)(2,1)} fusion(bf16[128,4096]{1,0:T(8,128)(2,1)} %all-gather.3.cloned.1.call-done, s32[2048]{0:T(1024)S(1)} %pad_clamp_fusion.1), kind=kCustom, calls=%fused_computation | custom fusion | bytes 25171968 | tf_op jit(solution)/shard_map/gather | solution.py:32
  61.6 6.3 broadcast_select_fusion
  67.9 288.5 %all_to_all.44 = bf16[64,24,4096]{2,1,0:T(8,128)(2,1)S(1)} all-to-all(bf16[64,24,4096]{2,1,0:T(8,128)(2,1)S(1)} %broadcast_select_fusion), channel_id=1, replica_groups=mesh['expert'=64,'hidden'=4] {'expert'}, dimensions={0} | all-to-all | bytes 25165824 | tf_op jit(solution)/shard_map/all_to_all | solution.py:41
  356.4 4.3 fusion.17
  360.7 5.2 fusion.13
  365.9 2.4 all_to_all.32
  368.3 1.9 copy.35
  370.2 39.1 %all_to_all.45 = bf16[192,4,1024]{2,0,1:T(8,128)(2,1)} all-to-all(bf16[192,4,1024]{2,0,1:T(8,128)(2,1)S(1)} %copy.35), channel_id=1, replica_groups=mesh['expert'=64,'hidden'=4] {'hidden'}, dimensions={1} | all-to-all | bytes 3145728 | tf_op jit(solution)/shard_map/all_to_all | solution.py:48
  409.3 4.1 all-gather.5.cloned.1.call-done
  413.4 6.5 convolution_convert_fusion
  419.9 6.0 all-to-all-start.2
  426.4 73.0 %all-to-all-done.2 = bf16[64,24,1024]{2,1,0:T(8,128)(2,1)} async-done(((bf16[64,24,1024]{2,1,0:T(8,128)(2,1)}), bf16[64,24,1024]{2,1,0:T(8,128)(2,1)}, u32[]{:S(2)}, u32[]{:S(2)}) %all-to-all-start.2) | async-done | bytes 3145760 | tf_op jit(solution)/shard_map/all_to_all | solution.py:52
  499.4 8.4 %gather_fusion.1 = bf16[1024,1024]{1,0:T(8,128)(2,1)} fusion(bf16[1536,1024]{1,0:T(8,128)(2,1)} %bitcast.15, s32[1024]{0:T(1024)S(1)} %broadcast_clamp_fusion), kind=kCustom, calls=%fused_computation.1 | custom fusion | bytes 4198400 | tf_op jit(solution)/shard_map/gather | solution.py:55
  507.7 2.3 fusion.14
  510.2 1.7 fusion
  511.9 9.7 %gather_fusion.2 = bf16[1536,1024]{1,0:T(8,128)(2,1)} fusion(bf16[1024,1024]{1,0:T(8,128)(2,1)} %fusion, s32[2048]{0:T(1024)S(1)} %pad_clamp_fusion), kind=kCustom, calls=%fused_computation.2 | custom fusion | bytes 6297600 | tf_op jit(solution)/shard_map/gather | solution.py:32
  521.5 2.1 broadcast_select_fusion.1
  523.6 79.1 %all_to_all.46 = bf16[64,24,1024]{2,1,0:T(8,128)(2,1)S(1)} all-to-all(bf16[64,24,1024]{2,1,0:T(8,128)(2,1)S(1)} %broadcast_select_fusion.1), channel_id=1, replica_groups=mesh['expert'=64,'hidden'=4] {'expert'}, dimensions={0} | all-to-all | bytes 6291456 | tf_op jit(solution)/shard_map/all_to_all | solution.py:62
  602.8 4.3 fusion.30
  607.0 4.6 all-to-all-start.4
  612.3 37.1 %all-to-all-done.4 = f32[4,192,1024]{2,1,0:T(8,128)} async-done(((f32[4,192,1024]{2,1,0:T(8,128)}), f32[4,192,1024]{2,1,0:T(8,128)}, u32[]{:S(2)}, u32[]{:S(2)}) %all-to-all-start.4) | async-done | bytes 3145760 | tf_op jit(solution)/shard_map/all_to_all | solution.py:68
  649.4 4.6 fusion.21
  655.6 1.6 fusion.5
  657.2 74.2 %all-reduce = (f32[]{:T(128)}, f32[]{:T(128)}) all-reduce(f32[]{:T(128)} %get-tuple-element.12, f32[]{:T(128)} %get-tuple-element.13), channel_id=1, replica_groups=mesh['expert'=64,'hidden'=4] {'expert','hidden'}, use_global_device_ids=true, to_apply=%region_1.2 | all-reduce | flops 2 | bytes 16 | tf_op jit(solution)/shard_map/psum | solution.py:72
  732.7 3.3 fusion.7
  736.0 74.3 %psum.23 = f32[]{:T(128)} all-reduce(f32[]{:T(128)} %fusion.7), channel_id=1, replica_groups=mesh['expert'=64,'hidden'=4] {'expert','hidden'}, use_global_device_ids=true, to_apply=%region_9.10 | all-reduce | flops 1 | bytes 8 | tf_op jit(solution)/shard_map/psum | solution.py:77
  811.6 5.6 copy.36
  817.3 5.4 div.56
  822.6 5.3 fusion.12
  (49 shorter events, 5.5 us)
Async XLA Ops:
  7.2 349.3 %copy-start = (bf16[1,4096,192]{1,2,0:T(8,128)(2,1)S(1)}, bf16[1,4096,192]{1,2,0:T(8,128)(2,1)}, u32[]{:S(2)}) copy-start(bf16[1,4096,192]{1,2,0:T(8,128)(2,1)} %param.14) | copy-start | bytes 4718596
  7.2 31.0 %all-gather.3.cloned.1.call-start = ((), (), s32[]{:S(2)}) async-start(), calls=%async_computation.5 | async-start | bytes 1310720 | tf_op jit(solution)/shard_map/all_gather | solution.py:39
  7.9 405.5 %all-gather.5.cloned.1.call-start = ((), (), s32[]{:S(2)}) async-start(), calls=%async_computation.6 | async-start | bytes 2949120 | tf_op jit(solution)/shard_map/all_gather | solution.py:47
  356.4 4.3 copy-start.8
  360.7 5.2 copy-start.3
  419.9 6.1 copy-start.5
  419.9 79.4 %all-to-all-start.2 = ((bf16[64,24,1024]{2,1,0:T(8,128)(2,1)}), bf16[64,24,1024]{2,1,0:T(8,128)(2,1)}, u32[]{:S(2)}, u32[]{:S(2)}) async-start(bf16[64,24,1024]{2,1,0:T(8,128)(2,1)} %bitcast.94), calls=%async_computation.2 | async-start | bytes 6291456 | tf_op jit(solution)/shard_map/all_to_all | solution.py:52
  499.4 10.6 %copy-start.6 = (f32[128]{0:T(128)S(1)}, f32[128]{0:T(128)}, u32[]{:S(2)}) copy-start(f32[128]{0:T(128)} %param.12) | copy-start | bytes 1540
  523.6 79.2 %copy-start.7 = (bf16[1536,768]{0,1:T(8,128)(2,1)S(1)}, bf16[1536,768]{0,1:T(8,128)(2,1)}, u32[]{:S(2)}) copy-start(bf16[1536,768]{0,1:T(8,128)(2,1)} %all-gather.5.cloned.1.call-done) | copy-start | bytes 7077892
  607.0 42.4 %all-to-all-start.4 = ((f32[4,192,1024]{2,1,0:T(8,128)}), f32[4,192,1024]{2,1,0:T(8,128)}, u32[]{:S(2)}, u32[]{:S(2)}) async-start(f32[4,192,1024]{2,1,0:T(8,128)} %fusion.30), calls=%async_computation.4 | async-start | bytes 6291456 | tf_op jit(solution)/shard_map/all_to_all | solution.py:68
  654.0 1.6 copy-start.4
  654.4 2.7 copy-start.2
  817.3 10.7 %copy-start.1 = (bf16[1,4096,192]{1,2,0:T(8,128)(2,1)S(1)}, bf16[1,4096,192]{1,2,0:T(8,128)(2,1)}, u32[]{:S(2)}) copy-start(bf16[1,4096,192]{1,2,0:T(8,128)(2,1)} %param.14) | copy-start | bytes 4718596
Sparse Core Ops, SparseCore 0:
  9.8 28.3 all-gather.2
  366.1 47.3 all-gather.4
where the time goes:
time: 836 us; the launch traced here: 835 us
  blocking collectives  555 us (66%)
  waiting for transfers between devices  120 us (14%)
  local copies, waits for them, and re-layouts  64.5 us (8%)
  other arithmetic  44 us (5%)
  matrix products  22.5 us (3%)
  between operations  17.6 us (2%)
  starting transfers between devices  10.8 us (1%)
    all_to_all x1, blocking collectives, per_device(): lax.all_to_all(send_rows, 'expert', split_axis=0, concat_axis=0, tiled=True)  289 us
    all_to_all x1, blocking collectives, per_device(): lax.all_to_all(send_back, 'expert', split_axis=0, concat_axis=0, tiled=True)  79.1 us
    psum x1, blocking collectives, per_device(): rr_new = lax.psum(jnp.sum(updated * updated), ('expert', 'hidden'))  74.3 us
    psum x1, blocking collectives, per_device(): lax.psum((jnp.sum(search * image), jnp.sum(resid * resid)), ('expert', 'h...  74.2 us
    all_to_all x1, waiting for transfers between devices, per_device(): lax.all_to_all(tangent.reshape(experts, capacity, -1), 'expert', split_ax...  73 us
    all_to_all x1, blocking collectives, per_device(): lax.all_to_all(direction[0], 'hidden', split_axis=1, concat_axis=0, tiled...  39.1 us
    all_to_all x1, waiting for transfers between devices, per_device(): lax.all_to_all(curvature_cols, 'hidden', split_axis=0, concat_axis=1, til...  37.1 us
    gather x2, local copies, waits for them, and re-layouts, pack_rows(): picked = source_rows[index]  33 us
  transfers between devices with their start and end apart: 4, of which 4 were waited for; matrix products, arithmetic and copies ran while one was open for 3% of the time, Pallas kernels for 0%

commit v1 on v0

--- a/solution.py
+++ b/solution.py
@@ -70,7 +70,7 @@
     resid = residual[0].astype(jnp.float32)
     image = search + curvature / damping[0]
     pq_total, rr_total = lax.psum(
-        (jnp.sum(search * image), jnp.sum(resid * resid)), ("expert", "hidden")
+        lax.psum((jnp.sum(search * image), jnp.sum(resid * resid)), "hidden"), "expert"
     )
     alpha_step = rr_total / pq_total
     updated = resid - alpha_step * image

time: 836 us -> 894 us (1.069)
  blocking collectives: 555 us -> 614 us
    psum x1 -> x2, blocking collectives: 74.2 us -> 134 us  [the longest x1 127 us: per_device(): lax.psum(lax.psum((jnp.sum(search * image), jnp.sum(resid * resid)), 'hid...]
where the time goes in v1:
time: 894 us; the launch traced here: 893 us
  blocking collectives  614 us (69%)
  waiting for transfers between devices  120 us (13%)
  local copies, waits for them, and re-layouts  64.5 us (7%)
  other arithmetic  44 us (5%)
  matrix products  22.5 us (3%)
  between operations  17.6 us (2%)
  starting transfers between devices  10.8 us (1%)
    all_to_all x1, blocking collectives, per_device(): lax.all_to_all(send_rows, 'expert', split_axis=0, concat_axis=0, tiled=True)  289 us
    psum x1, blocking collectives, per_device(): lax.psum(lax.psum((jnp.sum(search * image), jnp.sum(resid * resid)), 'hid...  127 us
    all_to_all x1, blocking collectives, per_device(): lax.all_to_all(send_back, 'expert', split_axis=0, concat_axis=0, tiled=True)  79.1 us
    all_to_all x1, waiting for transfers between devices, per_device(): lax.all_to_all(tangent.reshape(experts, capacity, -1), 'expert', split_ax...  73 us
    psum x1, blocking collectives, per_device(): rr_new = lax.psum(jnp.sum(updated * updated), ('expert', 'hidden'))  72.8 us
    all_to_all x1, blocking collectives, per_device(): lax.all_to_all(direction[0], 'hidden', split_axis=1, concat_axis=0, tiled...  39.1 us
    all_to_all x1, waiting for transfers between devices, per_device(): lax.all_to_all(curvature_cols, 'hidden', split_axis=0, concat_axis=1, til...  37.1 us
    gather x2, local copies, waits for them, and re-layouts, pack_rows(): picked = source_rows[index]  33 us
  transfers between devices with their start and end apart: 4, of which 4 were waited for; matrix products, arithmetic and copies ran while one was open for 3% of the time, Pallas kernels for 0%

profile of v1, /device:TPU:1, one launch (start us, length us, event | category | flops | bytes accessed | tf_op | source)
XLA Modules:
  0.0 893.4 jit_solution(12705190566117615908)
XLA Ops:
  9.0 18.0 %reduce-window.6 = s32[64,8,128]{2,1,0:T(8,128)S(1)} reduce-window(s32[64,8,128]{2,1,0:T(8,128)S(1)} %fusion.25, s32[]{:T(128)} %constant.30.clone.1), window={size=1x1x128 pad=0_0x0_0x127_0}, to_apply=%region_3.4 | reduce-window | flops 8323072 | bytes 524292 | tf_op jit(solution)/shard_map/reduce-window
  28.5 4.3 scatter_custom_fusion
  33.0 5.2 all-gather.3.cloned.1.call-done
  38.2 23.4 %gather_fusion = bf16[1536,4096]{1,0:T(8,128)(2,1)} fusion(bf16[128,4096]{1,0:T(8,128)(2,1)} %all-gather.3.cloned.1.call-done, s32[2048]{0:T(1024)S(1)} %pad_clamp_fusion.1), kind=kCustom, calls=%fused_computation | custom fusion | bytes 25171968 | tf_op jit(solution)/shard_map/gather | solution.py:32
  61.6 6.3 broadcast_select_fusion
  67.9 288.5 %all_to_all.44 = bf16[64,24,4096]{2,1,0:T(8,128)(2,1)S(1)} all-to-all(bf16[64,24,4096]{2,1,0:T(8,128)(2,1)S(1)} %broadcast_select_fusion), channel_id=1, replica_groups=mesh['expert'=64,'hidden'=4] {'expert'}, dimensions={0} | all-to-all | bytes 25165824 | tf_op jit(solution)/shard_map/all_to_all | solution.py:41
  356.4 4.3 fusion.17
  360.7 5.2 fusion.13
  365.9 2.4 all_to_all.32
  368.3 1.9 copy.35
  370.2 39.1 %all_to_all.45 = bf16[192,4,1024]{2,0,1:T(8,128)(2,1)} all-to-all(bf16[192,4,1024]{2,0,1:T(8,128)(2,1)S(1)} %copy.35), channel_id=1, replica_groups=mesh['expert'=64,'hidden'=4] {'hidden'}, dimensions={1} | all-to-all | bytes 3145728 | tf_op jit(solution)/shard_map/all_to_all | solution.py:48
  409.3 4.1 all-gather.5.cloned.1.call-done
  413.4 6.5 convolution_convert_fusion
  419.9 6.0 all-to-all-start.2
  426.4 73.0 %all-to-all-done.2 = bf16[64,24,1024]{2,1,0:T(8,128)(2,1)} async-done(((bf16[64,24,1024]{2,1,0:T(8,128)(2,1)}), bf16[64,24,1024]{2,1,0:T(8,128)(2,1)}, u32[]{:S(2)}, u32[]{:S(2)}) %all-to-all-start.2) | async-done | bytes 3145760 | tf_op jit(solution)/shard_map/all_to_all | solution.py:52
  499.4 8.4 gather_fusion.1
  507.7 2.3 fusion.14
  510.2 1.7 fusion
  511.9 9.7 %gather_fusion.2 = bf16[1536,1024]{1,0:T(8,128)(2,1)} fusion(bf16[1024,1024]{1,0:T(8,128)(2,1)} %fusion, s32[2048]{0:T(1024)S(1)} %pad_clamp_fusion), kind=kCustom, calls=%fused_computation.2 | custom fusion | bytes 6297600 | tf_op jit(solution)/shard_map/gather | solution.py:32
  521.5 2.1 broadcast_select_fusion.1
  523.6 79.1 %all_to_all.46 = bf16[64,24,1024]{2,1,0:T(8,128)(2,1)S(1)} all-to-all(bf16[64,24,1024]{2,1,0:T(8,128)(2,1)S(1)} %broadcast_select_fusion.1), channel_id=1, replica_groups=mesh['expert'=64,'hidden'=4] {'expert'}, dimensions={0} | all-to-all | bytes 6291456 | tf_op jit(solution)/shard_map/all_to_all | solution.py:62
  602.8 4.3 fusion.30
  607.0 4.6 all-to-all-start.4
  612.3 37.1 %all-to-all-done.4 = f32[4,192,1024]{2,1,0:T(8,128)} async-done(((f32[4,192,1024]{2,1,0:T(8,128)}), f32[4,192,1024]{2,1,0:T(8,128)}, u32[]{:S(2)}, u32[]{:S(2)}) %all-to-all-start.4) | async-done | bytes 3145760 | tf_op jit(solution)/shard_map/all_to_all | solution.py:68
  649.4 4.6 fusion.21
  657.2 7.5 all-reduce.1
  664.6 126.9 %all-reduce = (f32[]{:T(128)}, f32[]{:T(128)}) all-reduce(f32[]{:T(128)} %get-tuple-element.5, f32[]{:T(128)} %get-tuple-element.6), channel_id=1, replica_groups=mesh['expert'=64,'hidden'=4] {'expert'}, use_global_device_ids=true, to_apply=%region_2.3 | all-reduce | flops 2 | bytes 16 | tf_op jit(solution)/shard_map/psum | solution.py:72
  792.9 3.3 fusion.7
  796.2 72.8 %psum.39 = f32[]{:T(128)} all-reduce(f32[]{:T(128)} %fusion.7), channel_id=1, replica_groups=mesh['expert'=64,'hidden'=4] {'expert','hidden'}, use_global_device_ids=true, to_apply=%region_11.12 | all-reduce | flops 1 | bytes 8 | tf_op jit(solution)/shard_map/psum | solution.py:77
  870.3 5.6 copy.36
  875.9 5.4 div.56
  881.3 5.3 fusion.12
  (50 shorter events, 7.0 us)
Async XLA Ops:
  7.2 349.3 %copy-start = (bf16[1,4096,192]{1,2,0:T(8,128)(2,1)S(1)}, bf16[1,4096,192]{1,2,0:T(8,128)(2,1)}, u32[]{:S(2)}) copy-start(bf16[1,4096,192]{1,2,0:T(8,128)(2,1)} %param.14) | copy-start | bytes 4718596
  7.2 31.0 %all-gather.3.cloned.1.call-start = ((), (), s32[]{:S(2)}) async-start(), calls=%async_computation.5 | async-start | bytes 1310720 | tf_op jit(solution)/shard_map/all_gather | solution.py:39
  7.9 405.5 %all-gather.5.cloned.1.call-start = ((), (), s32[]{:S(2)}) async-start(), calls=%async_computation.6 | async-start | bytes 2949120 | tf_op jit(solution)/shard_map/all_gather | solution.py:47
  356.4 4.3 copy-start.8
  360.7 5.2 copy-start.3
  419.9 6.1 copy-start.5
  419.9 79.4 %all-to-all-start.2 = ((bf16[64,24,1024]{2,1,0:T(8,128)(2,1)}), bf16[64,24,1024]{2,1,0:T(8,128)(2,1)}, u32[]{:S(2)}, u32[]{:S(2)}) async-start(bf16[64,24,1024]{2,1,0:T(8,128)(2,1)} %bitcast.94), calls=%async_computation.2 | async-start | bytes 6291456 | tf_op jit(solution)/shard_map/all_to_all | solution.py:52
  499.4 10.6 %copy-start.6 = (f32[128]{0:T(128)S(1)}, f32[128]{0:T(128)}, u32[]{:S(2)}) copy-start(f32[128]{0:T(128)} %param.12) | copy-start | bytes 1540
  523.6 79.2 %copy-start.7 = (bf16[1536,768]{0,1:T(8,128)(2,1)S(1)}, bf16[1536,768]{0,1:T(8,128)(2,1)}, u32[]{:S(2)}) copy-start(bf16[1536,768]{0,1:T(8,128)(2,1)} %all-gather.5.cloned.1.call-done) | copy-start | bytes 7077892
  607.0 42.4 %all-to-all-start.4 = ((f32[4,192,1024]{2,1,0:T(8,128)}), f32[4,192,1024]{2,1,0:T(8,128)}, u32[]{:S(2)}, u32[]{:S(2)}) async-start(f32[4,192,1024]{2,1,0:T(8,128)} %fusion.30), calls=%async_computation.4 | async-start | bytes 6291456 | tf_op jit(solution)/shard_map/all_to_all | solution.py:68
  654.0 1.6 copy-start.4
  654.4 2.7 copy-start.2
  875.9 10.7 %copy-start.1 = (bf16[1,4096,192]{1,2,0:T(8,128)(2,1)S(1)}, bf16[1,4096,192]{1,2,0:T(8,128)(2,1)}, u32[]{:S(2)}) copy-start(bf16[1,4096,192]{1,2,0:T(8,128)(2,1)} %param.14) | copy-start | bytes 4718596
Sparse Core Ops, SparseCore 0:
  9.8 28.3 all-gather.2
  366.1 47.3 all-gather.4
